TPU v7x, 32 devices: a whole 2x2x4 slice. The times are simulated.
32 devices in a mesh: seq: 8 (over z, y), mp: 4 (over x, core).
Axes of the slice: x: 2, y: 2, z: 4, core: 2. Of those that a mesh axis runs over, the one named last changes fastest.
Arguments:
- tokens: bfloat16 [16384, 2048], P('seq'), may hold values from -6 to 6
- w_proj: bfloat16 [2048, 4, 2048], P(None, None, 'mp')
- gain: float32 [2048], P('mp'), may hold values from 0.25 to 1.75
- level_codes: int32 [9, 16, 16384], P(None, 'mp', 'seq'), may hold values from 0 to 255
- w_codes: int32 [2048, 2048], P('mp'), may hold values from 40 to 199, as said below
- block_exponent: int32 [16, 16], P('mp'), may hold values from -7 to -5
Outputs:
- mixed: bfloat16 [16384, 2048], P(('seq', 'mp'))
Inputs may be any that keep to these rules, and one draw needn't show every extreme that they name: `w_codes`: each code is 128 s + 8 e + m with s of 0 or 1, e from 5 to 8 and m from 0 to 7.
All inputs are finite; a program needn't handle non-finite values.
Results may differ from a plain program's by a relative error of at most 0.015.
Values may be sent and summed in bfloat16 or wider, within the bound.
A program may use at most 128 MiB of HBM per device.

v0:
```python
import functools
import math

import jax
import jax.numpy as jnp
from jax import lax
from jax.experimental import pallas as pl
from jax.experimental.pallas import tpu as pltpu
from jax.sharding import PartitionSpec as P

HEAD_DIM = 128
STRETCH = 64
BLOCK = 128
CORES = 2
QB = 256
MESH = pl.DeviceIdType.MESH
F32 = jnp.float32
BF16 = jnp.bfloat16


def power_of_two(field, bits):
    result = jnp.ones(field.shape, jnp.float32)
    for bit in range(bits):
        result = result * jnp.where(
            field // 2**bit % 2 == 1, jnp.float32(2.0**2**bit), jnp.float32(1.0)
        )
    return result


def dot(a, b):
    return jnp.dot(a, b, preferred_element_type=F32)


def dot_nt(a, b):
    return lax.dot_general(a, b, (((1,), (1,)), ((), ())), preferred_element_type=F32)


def dot_tn(a, b):
    return lax.dot_general(a, b, (((0,), (0,)), ((), ())), preferred_element_type=F32)


def kernel(
    cfg,
    tok_hbm, w_hbm, codes_hbm, gain_ref, lw_ref, scale_ref,
    out_ref,
    tok, wj, wstage, cstage, wfull, kv, q, gate, att, attr, local, tot, snd, rcv, masks, acc,
    tok_sem, w_sem, c_sem, ws_sem, wr_sem, as_sem, ar_sem, ss_sem, sr_sem,
):
    groups, seq_bits, block_bits, in_bits = cfg
    rows_all, width = q.shape
    depth = tok.shape[1]
    heads = width // HEAD_DIM
    rows = rows_all // groups
    chips = groups // CORES
    seq = lax.axis_index("seq")
    mp = lax.axis_index("mp")
    x = mp // CORES
    c = mp % CORES

    def peer(ix, kc):
        return ((x + ix) % chips) * CORES + (c + kc) % CORES

    def source(ix, kc):
        return ((x - ix + chips) % chips) * CORES + (c - kc + CORES) % CORES

    def seq_peer(j):
        bit = (seq // 2**j) % 2
        return seq + 2**j - bit * 2 ** (j + 1)

    crows = cstage.shape[1]
    wrows = wstage.shape[1]
    n_c = width // crows
    n_w = depth // wrows

    def c_copy(i):
        slot = i % 2
        return pltpu.make_async_copy(
            codes_hbm.at[pl.ds(i * crows, crows)], cstage.at[slot], c_sem.at[slot]
        )

    def w_copy(i):
        slot = i % 2
        return pltpu.make_async_copy(
            w_hbm.at[pl.ds(i * wrows, wrows)], wstage.at[slot], w_sem.at[slot]
        )

    for i in range(2):
        c_copy(i).start()
    for i in range(2):
        w_copy(i).start()
    tok_copy = pltpu.make_async_copy(tok_hbm, tok, tok_sem)
    tok_copy.start()

    barrier = pltpu.get_barrier_semaphore()
    for r in range(1, groups):
        pl.semaphore_signal(
            barrier, inc=1, device_id=(seq, peer(r // CORES, r % CORES)), device_id_type=MESH
        )
    for j in range(seq_bits):
        pl.semaphore_signal(barrier, inc=1, device_id=(seq_peer(j), mp), device_id_type=MESH)

    @pl.loop(0, n_c)
    def _(i):
        c_copy(i).wait()
        codes = cstage[i % 2]
        whole = ((codes & 7) | 8) << ((codes >> 3) & 15)
        value = whole.astype(F32)
        value = jnp.where(codes >= 128, -value, value) * scale_ref[pl.ds(i, 1), :]
        wfull[mp, pl.ds(pl.multiple_of(i * crows, crows), crows), :] = value.astype(BF16)

        @pl.when(i + 2 < n_c)
        def _():
            c_copy(i + 2).start()

    t = lax.broadcasted_iota(jnp.int32, (QB, QB), 0)
    s = lax.broadcasted_iota(jnp.int32, (QB, QB), 1)
    tc = t // STRETCH
    sc = s // STRETCH
    masks[0] = jnp.where((tc == sc) & (s <= t), 1.0, 0.0).astype(F32)
    for j in range(in_bits):
        hit = ((tc // 2**j) % 2 == 1) & (sc // 2**j == tc // 2**j - 1)
        masks[j + 1] = jnp.where(hit, 1.0, 0.0).astype(F32)

    pl.semaphore_wait(barrier, groups - 1 + seq_bits)

    def w_send(k, shard, target):
        return pltpu.make_async_remote_copy(
            src_ref=wfull.at[shard], dst_ref=wfull.at[shard],
            send_sem=ws_sem.at[k], recv_sem=wr_sem.at[k],
            device_id=(seq, target), device_id_type=MESH,
        )

    for ix in range(1, chips):
        w_send(ix, mp, peer(ix, 0)).start()
    w_send(0, mp, peer(0, 1)).start()

    @pl.loop(0, n_w)
    def _(i):
        w_copy(i).wait()
        wj[:, pl.ds(pl.multiple_of(i * wrows, wrows), wrows), :] = jnp.swapaxes(wstage[i % 2], 0, 1)

        @pl.when(i + 2 < n_w)
        def _():
            w_copy(i + 2).start()

    tok_copy.wait()
    tb = min(512, rows_all)
    n_t = rows_all // tb

    @pl.loop(0, 2 * n_t)
    def _(i):
        part = i // n_t
        at = pl.ds(pl.multiple_of((i % n_t) * tb, tb), tb)
        kv[part, at, :] = dot(tok[at, :], wj[1 + part]).astype(BF16)

    n_b = rows_all // QB

    @pl.loop(0, heads)
    def _(h):
        cols = pl.ds(pl.multiple_of(h * HEAD_DIM, HEAD_DIM), HEAD_DIM)
        level = []
        for b in range(n_b):
            at = pl.ds(b * QB, QB)
            level.append(dot_tn(kv[0, at, cols], kv[1, at, cols]))
        base = 0
        while len(level) > 1:
            for b, state in enumerate(level):
                local[base + b, h] = state.astype(BF16)
            base += len(level)
            level = [level[2 * b] + level[2 * b + 1] for b in range(len(level) // 2)]
        tot[h] = level[0]
        snd[0, h] = level[0].astype(BF16)

    def s_send(j):
        return pltpu.make_async_remote_copy(
            src_ref=snd.at[j], dst_ref=rcv.at[j],
            send_sem=ss_sem.at[j], recv_sem=sr_sem.at[j],
            device_id=(seq_peer(j), mp), device_id_type=MESH,
        )

    s_send(0).start()

    def exchange(j):
        s_send(j).wait_recv()
        if j + 1 < seq_bits:
            total = tot[...] + rcv[j].astype(F32)
            tot[...] = total
            snd[j + 1] = total.astype(BF16)
            s_send(j + 1).start()

    @pl.loop(0, n_t)
    def _(i):
        at = pl.ds(pl.multiple_of(i * tb, tb), tb)
        q[at, :] = dot(tok[at, :], wj[0]).astype(BF16)
        g = dot(tok[at, :], wj[3])
        gate[at, :] = g / (1.0 + jnp.exp(-g)) * gain_ref[...]
        for j in range(min(seq_bits, n_t)):
            @pl.when(i == j)
            def _(j=j):
                exchange(j)

    for j in range(n_t, seq_bits):
        exchange(j)

    def a_send(r, target):
        at = pl.ds(pl.multiple_of(target * rows, rows), rows)
        return pltpu.make_async_remote_copy(
            src_ref=att.at[at], dst_ref=attr.at[mp],
            send_sem=as_sem.at[r], recv_sem=ar_sem.at[r],
            device_id=(seq, target), device_id_type=MESH,
        )

    n_in = 1 + in_bits

    @pl.loop(0, groups)
    def _(step):
        r = groups - 1 - step
        owner = peer(r // CORES, r % CORES)

        @pl.loop(0, rows // QB)
        def _(part):
            b = owner * (rows // QB) + part
            at = pl.ds(pl.multiple_of(b * QB, QB), QB)
            for h in range(heads):
                cols = slice(h * HEAD_DIM, (h + 1) * HEAD_DIM)
                qh = q[at, cols]

                def weight(level):
                    k = level * heads + h
                    return lw_ref[at, k : k + 1]

                scores = dot_nt(qh, kv[0, at, cols])
                mix = weight(0) * masks[0]
                for j in range(in_bits):
                    mix = mix + weight(1 + j) * masks[1 + j]
                left = [(scores * mix).astype(BF16)]
                right = [kv[1, at, cols]]
                qf = qh.astype(F32)
                base = 0
                for j in range(block_bits):
                    node = b // 2**j
                    bit = node % 2
                    left.append((qf * (weight(n_in + j) * bit.astype(F32))).astype(BF16))
                    right.append(local[base + node - bit, h])
                    base += n_b >> j
                for j in range(seq_bits):
                    bit = (seq // 2**j) % 2
                    left.append((qf * (weight(n_in + block_bits + j) * bit.astype(F32))).astype(BF16))
                    right.append(rcv[j, h])
                memory = dot(jnp.concatenate(left, 1), jnp.concatenate(right, 0))
                mean = jnp.mean(memory * memory, axis=-1, keepdims=True)
                att[at, cols] = (memory * lax.rsqrt(mean + 1e-06) * gate[at, cols]).astype(BF16)

        @pl.when(r > 0)
        def _():
            a_send(r, owner).start()

    for ix in range(1, chips):
        shard = source(ix, 0)
        w_send(ix, shard, mp_other(x, c)).wait_recv()
        w_send(chips - 1 + ix, shard, peer(0, 1)).start()

    nb = min(512, depth)

    def product(left, g, first, last):
        @pl.loop(0, depth // nb)
        def _(i):
            cols = pl.ds(pl.multiple_of(i * nb, nb), nb)
            value = dot(left, wfull[g, :, cols])
            if not first:
                value = value + acc[:, cols]
            if last:
                out_ref[:, cols] = value.astype(BF16)
            else:
                acc[:, cols] = value

    own = pl.ds(pl.multiple_of(mp * rows, rows), rows)
    product(att[own, :], mp, True, groups == 1)
    for r in range(1, groups):
        ix, kc = r // CORES, r % CORES
        src = source(ix, kc)
        at = pl.ds(pl.multiple_of(src * rows, rows), rows)
        pltpu.make_async_remote_copy(
            src_ref=att.at[own], dst_ref=attr.at[src],
            send_sem=as_sem.at[r], recv_sem=ar_sem.at[r],
            device_id=(seq, src), device_id_type=MESH,
        ).wait_recv()
        if kc:
            k = 0 if ix == 0 else chips - 1 + ix
            w_send(k, src, src).wait_recv()
        product(attr[src], src, False, r == groups - 1)

    w_send(0, mp, peer(0, 1)).wait_send()
    for ix in range(1, chips):
        w_send(ix, mp, peer(ix, 0)).wait_send()
        w_send(chips - 1 + ix, source(ix, 0), peer(0, 1)).wait_send()
    for j in range(seq_bits):
        s_send(j).wait_send()
    for r in range(1, groups):
        a_send(r, peer(r // CORES, r % CORES)).wait_send()


def mp_other(x, c):
    return x * CORES + (c + 1) % CORES


def body(tokens, w_proj, gain, level_codes, w_codes, block_exponent):
    rows_all, depth = tokens.shape
    width = w_proj.shape[2]
    heads = width // HEAD_DIM
    groups = lax.axis_size("mp")
    seq_size = lax.axis_size("seq")
    seq_bits = seq_size.bit_length() - 1
    stretch_bits = (rows_all // STRETCH).bit_length() - 1
    in_bits = (QB // STRETCH).bit_length() - 1
    block_bits = stretch_bits - in_bits
    levels = level_codes.shape[0]
    rows = rows_all // groups
    chips = groups // CORES
    spans = [STRETCH] + [STRETCH << j for j in range(levels - 1)]
    factors = jnp.array([1.0 / 128.0 / math.sqrt(HEAD_DIM * span) for span in spans], F32)
    level_weight = (level_codes.astype(F32) * factors[:, None, None]).reshape(
        levels * heads, rows_all
    ).T
    scales = power_of_two(block_exponent + 16, 5) * jnp.float32(2.0 ** (-26))
    scales = jnp.repeat(scales, BLOCK, axis=1)
    n_b = rows_all // QB
    vmem = pl.BlockSpec(memory_space=pltpu.VMEM)
    hbm = pl.BlockSpec(memory_space=pl.ANY)
    dma = pltpu.SemaphoreType.DMA
    return pl.pallas_call(
        functools.partial(kernel, (groups, seq_bits, block_bits, in_bits)),
        out_shape=jax.ShapeDtypeStruct((rows, depth), BF16),
        in_specs=[hbm, hbm, hbm, vmem, vmem, vmem],
        out_specs=vmem,
        scratch_shapes=[
            pltpu.VMEM((rows_all, depth), BF16),
            pltpu.VMEM((4, depth, width), BF16),
            pltpu.VMEM((2, 256, 4, width), BF16),
            pltpu.VMEM((2, BLOCK, depth), jnp.int32),
            pltpu.VMEM((groups, width, depth), BF16),
            pltpu.VMEM((2, rows_all, width), BF16),
            pltpu.VMEM((rows_all, width), BF16),
            pltpu.VMEM((rows_all, width), F32),
            pltpu.VMEM((rows_all, width), BF16),
            pltpu.VMEM((groups, rows, width), BF16),
            pltpu.VMEM((2 * n_b, heads, HEAD_DIM, HEAD_DIM), BF16),
            pltpu.VMEM((heads, HEAD_DIM, HEAD_DIM), F32),
            pltpu.VMEM((seq_bits, heads, HEAD_DIM, HEAD_DIM), BF16),
            pltpu.VMEM((seq_bits, heads, HEAD_DIM, HEAD_DIM), BF16),
            pltpu.VMEM((1 + in_bits, QB, QB), F32),
            pltpu.VMEM((rows, depth), F32),
            dma, dma((2,)), dma((2,)),
            dma((2 * chips - 1,)), dma((2 * chips - 1,)),
            dma((groups,)), dma((groups,)),
            dma((seq_bits,)), dma((seq_bits,)),
        ],
        compiler_params=pltpu.CompilerParams(
            collective_id=0, has_side_effects=True, vmem_limit_bytes=67043328
        ),
        name="layer",
    )(tokens, w_proj, w_codes, gain.reshape(1, width), level_weight, scales)


def solution(mesh):
    placed = (
        P("seq", None),
        P(None, None, "mp"),
        P("mp"),
        P(None, "mp", "seq"),
        P("mp", None),
        P("mp", None),
    )
    return jax.shard_map(
        body, mesh=mesh, in_specs=placed, out_specs=P(("seq", "mp"), None), check_vma=False
    )
```

profile of v0, /device:TPU:0, one launch (start us, length us, event | category | flops | bytes accessed | tf_op | source)
XLA Modules:
  0.0 90.5 jit_solution(10587534326959869024)
XLA Ops:
  0.0 0.7 multiply_multiply_fusion
  0.7 0.1 broadcast_bitcast_fusion
  0.8 0.6 copy.12
  1.4 1.1 %convert_multiply_fusion = f32[9,4,2048]{2,1,0:T(4,128)S(1)} fusion(s32[9,4,2048]{2,1,0:T(4,128)} %param.10, f32[9]{0:T(128)} %constant.105.clone), kind=kLoop, calls=%fused_computation | loop fusion | flops 147456 | bytes 589860 | tf_op jit(solution)/shard_map/mul | solution.py:322
  2.5 0.1 reshape.11
  2.6 1.3 %copy.9 = f32[36,2048]{0,1:T(8,128)} copy(f32[36,2048]{1,0:T(8,128)S(1)} %reshape.11) | data formatting | bytes 589824 | tf_op jit(solution)/shard_map/reshape | solution.py:322
  3.9 83.4 %layer.1 = bf16[512,2048]{1,0:T(8,128)(2,1)} custom-call(bf16[2048,2048]{1,0:T(8,128)(2,1)} %tok_hbm.1, bf16[2048,4,512]{2,1,0:T(4,128)(2,1)} %w_hbm.1, s32[512,2048]{1,0:T(8,128)} %codes_hbm.1, f32[1,512]{1,0:T(1,128)} %bitcast.9, f32[2048,36]{1,0:T(8,128)} %bitcast.7, f32[4,2048]{1,0:T(4,128)} %bitcast.8), custom_call_target="tpu_custom_call" | custom-call | tf_op jit(solution)/shard_map/layer/pallas_call | solution.py:331
  87.3 3.2 %copy.14 = bf16[512,2048]{1,0:T(8,128)(2,1)} copy(bf16[512,2048]{1,0:T(8,128)(2,1)} %layer.1) | data formatting | bytes 4194304
where the time goes:
time: 90.8 us; the launch traced here: 90.5 us
  Pallas kernels  83.4 us (92%)
  local copies, waits for them, and re-layouts  5.29 us (6%)
  other arithmetic  1.78 us (2%)
    pallas_call x1, Pallas kernels, body(): pl.pallas_call(functools.partial(kernel, (groups, seq_bits, block_bits, i...  83.4 us
    unnamed x3, local copies, waits for them, and re-layouts  3.85 us

commit v1 on v0

--- a/solution.py
+++ b/solution.py
@@ -123,16 +123,46 @@
 
     pl.semaphore_wait(barrier, groups - 1 + seq_bits)
 
-    def w_send(k, shard, target):
+    n_x = chips - 1
+    parity = seq % 2
+    half = width // 2
+    piece = half // 2
+
+    def w_send(k, shard, start, size, seq_to, mp_to):
+        at = pl.ds(pl.multiple_of(start, piece), size)
         return pltpu.make_async_remote_copy(
-            src_ref=wfull.at[shard], dst_ref=wfull.at[shard],
+            src_ref=wfull.at[shard, at], dst_ref=wfull.at[shard, at],
             send_sem=ws_sem.at[k], recv_sem=wr_sem.at[k],
-            device_id=(seq, target), device_id_type=MESH,
-        )
-
-    for ix in range(1, chips):
-        w_send(ix, mp, peer(ix, 0)).start()
-    w_send(0, mp, peer(0, 1)).start()
+            device_id=(seq_to, mp_to), device_id_type=MESH,
+        )
+
+    def x_part(ix, ch, shard):
+        return w_send(2 * (ix - 1) + ch, shard, parity * half + ch * piece, piece, seq, peer(ix, 0))
+
+    def y_part(ix, ch, which):
+        k = 2 * n_x + 2 * (ix - 1) + ch
+        return w_send(k, source(ix, 0), which * half + ch * piece, piece, seq_peer(0), mp)
+
+    def cx_part(ix, ch, kc):
+        k = 4 * n_x + 2 * (ix - 1) + ch
+        return w_send(k, source(ix, kc), parity * half + ch * piece, piece, seq, peer(0, 1))
+
+    def cy_part(ix, kc):
+        return w_send(6 * n_x + ix - 1, source(ix, kc), (1 - parity) * half, half, seq, peer(0, 1))
+
+    def c_part(shard):
+        return w_send(7 * n_x, shard, 0, width, seq, peer(0, 1))
+
+    def relay(ch):
+        for ix in range(1, chips):
+            x_part(ix, ch, source(ix, 0)).wait_recv()
+            y_part(ix, ch, parity).start()
+            cx_part(ix, ch, 0).start()
+
+    for ch in range(2):
+        for ix in range(1, chips):
+            x_part(ix, ch, mp).start()
+    c_part(mp).start()
 
     @pl.loop(0, n_w)
     def _(i):
@@ -179,6 +209,7 @@
         )
 
     s_send(0).start()
+    relay(0)
 
     def exchange(j):
         s_send(j).wait_recv()
@@ -201,6 +232,8 @@
 
     for j in range(n_t, seq_bits):
         exchange(j)
+
+    relay(1)
 
     def a_send(r, target):
         at = pl.ds(pl.multiple_of(target * rows, rows), rows)
@@ -256,9 +289,9 @@
             a_send(r, owner).start()
 
     for ix in range(1, chips):
-        shard = source(ix, 0)
-        w_send(ix, shard, mp_other(x, c)).wait_recv()
-        w_send(chips - 1 + ix, shard, peer(0, 1)).start()
+        for ch in range(2):
+            y_part(ix, ch, 1 - parity).wait_recv()
+        cy_part(ix, 0).start()
 
     nb = min(512, depth)
 
@@ -285,23 +318,25 @@
             send_sem=as_sem.at[r], recv_sem=ar_sem.at[r],
             device_id=(seq, src), device_id_type=MESH,
         ).wait_recv()
-        if kc:
-            k = 0 if ix == 0 else chips - 1 + ix
-            w_send(k, src, src).wait_recv()
+        if kc and ix:
+            for ch in range(2):
+                cx_part(ix, ch, 1).wait_recv()
+            cy_part(ix, 1).wait_recv()
+        elif kc:
+            c_part(src).wait_recv()
         product(attr[src], src, False, r == groups - 1)
 
-    w_send(0, mp, peer(0, 1)).wait_send()
+    c_part(mp).wait_send()
     for ix in range(1, chips):
-        w_send(ix, mp, peer(ix, 0)).wait_send()
-        w_send(chips - 1 + ix, source(ix, 0), peer(0, 1)).wait_send()
+        for ch in range(2):
+            x_part(ix, ch, mp).wait_send()
+            y_part(ix, ch, parity).wait_send()
+            cx_part(ix, ch, 0).wait_send()
+        cy_part(ix, 0).wait_send()
     for j in range(seq_bits):
         s_send(j).wait_send()
     for r in range(1, groups):
         a_send(r, peer(r // CORES, r % CORES)).wait_send()
-
-
-def mp_other(x, c):
-    return x * CORES + (c + 1) % CORES
 
 
 def body(tokens, w_proj, gain, level_codes, w_codes, block_exponent):
@@ -351,7 +386,7 @@
             pltpu.VMEM((1 + in_bits, QB, QB), F32),
             pltpu.VMEM((rows, depth), F32),
             dma, dma((2,)), dma((2,)),
-            dma((2 * chips - 1,)), dma((2 * chips - 1,)),
+            dma((7 * chips - 6,)), dma((7 * chips - 6,)),
             dma((groups,)), dma((groups,)),
             dma((seq_bits,)), dma((seq_bits,)),
         ],

time: 90.8 us -> 84.3 us (0.928)
  Pallas kernels: 83.4 us -> 76.9 us
    pallas_call x1, Pallas kernels: 83.4 us -> 76.9 us  [body(): pl.pallas_call(functools.partial(kernel, (groups, seq_bits, block_bits, i...]
where the time goes in v1:
time: 84.3 us; the launch traced here: 84 us
  Pallas kernels  76.9 us (91%)
  local copies, waits for them, and re-layouts  5.29 us (6%)
  other arithmetic  1.78 us (2%)
    pallas_call x1, Pallas kernels, body(): pl.pallas_call(functools.partial(kernel, (groups, seq_bits, block_bits, i...  76.9 us
    unnamed x3, local copies, waits for them, and re-layouts  3.85 us

profile of v1, /device:TPU:0, one launch (start us, length us, event | category | flops | bytes accessed | tf_op | source)
XLA Modules:
  0.0 84.0 jit_solution(8497972101942880068)
XLA Ops:
  0.0 0.7 multiply_multiply_fusion
  0.7 0.1 broadcast_bitcast_fusion
  0.8 0.6 copy.12
  1.4 1.1 %convert_multiply_fusion = f32[9,4,2048]{2,1,0:T(4,128)S(1)} fusion(s32[9,4,2048]{2,1,0:T(4,128)} %param.10, f32[9]{0:T(128)} %constant.105.clone), kind=kLoop, calls=%fused_computation | loop fusion | flops 147456 | bytes 589860 | tf_op jit(solution)/shard_map/mul | solution.py:357
  2.5 0.1 reshape.11
  2.6 1.3 %copy.9 = f32[36,2048]{0,1:T(8,128)} copy(f32[36,2048]{1,0:T(8,128)S(1)} %reshape.11) | data formatting | bytes 589824 | tf_op jit(solution)/shard_map/reshape | solution.py:357
  3.9 76.9 %layer.1 = bf16[512,2048]{1,0:T(8,128)(2,1)} custom-call(bf16[2048,2048]{1,0:T(8,128)(2,1)} %tok_hbm.1, bf16[2048,4,512]{2,1,0:T(4,128)(2,1)} %w_hbm.1, s32[512,2048]{1,0:T(8,128)} %codes_hbm.1, f32[1,512]{1,0:T(1,128)} %bitcast.9, f32[2048,36]{1,0:T(8,128)} %bitcast.7, f32[4,2048]{1,0:T(4,128)} %bitcast.8), custom_call_target="tpu_custom_call" | custom-call | tf_op jit(solution)/shard_map/layer/pallas_call | solution.py:366
  80.9 3.2 %copy.14 = bf16[512,2048]{1,0:T(8,128)(2,1)} copy(bf16[512,2048]{1,0:T(8,128)(2,1)} %layer.1) | data formatting | bytes 4194304

commit v2 on v1

--- a/solution.py
+++ b/solution.py
@@ -18,15 +18,6 @@
 BF16 = jnp.bfloat16
 
 
-def power_of_two(field, bits):
-    result = jnp.ones(field.shape, jnp.float32)
-    for bit in range(bits):
-        result = result * jnp.where(
-            field // 2**bit % 2 == 1, jnp.float32(2.0**2**bit), jnp.float32(1.0)
-        )
-    return result
-
-
 def dot(a, b):
     return jnp.dot(a, b, preferred_element_type=F32)
 
@@ -46,7 +37,7 @@
     tok, wj, wstage, cstage, wfull, kv, q, gate, att, attr, local, tot, snd, rcv, masks, acc,
     tok_sem, w_sem, c_sem, ws_sem, wr_sem, as_sem, ar_sem, ss_sem, sr_sem,
 ):
-    groups, seq_bits, block_bits, in_bits = cfg
+    groups, seq_bits, block_bits, in_bits, factors = cfg
     rows_all, width = q.shape
     depth = tok.shape[1]
     heads = width // HEAD_DIM
@@ -105,19 +96,24 @@
         codes = cstage[i % 2]
         whole = ((codes & 7) | 8) << ((codes >> 3) & 15)
         value = whole.astype(F32)
-        value = jnp.where(codes >= 128, -value, value) * scale_ref[pl.ds(i, 1), :]
-        wfull[mp, pl.ds(pl.multiple_of(i * crows, crows), crows), :] = value.astype(BF16)
+        value = jnp.where(codes >= 128, -value, value)
+        at = pl.ds(pl.multiple_of(i * crows, crows), crows)
+        for k in range(depth // BLOCK):
+            scale = jnp.left_shift(jnp.int32(1), scale_ref[i, k] + 16).astype(F32) * 2.0**-26
+            cols = slice(k * BLOCK, (k + 1) * BLOCK)
+            wfull[mp, at, cols] = (value[:, cols] * scale).astype(BF16)
 
         @pl.when(i + 2 < n_c)
         def _():
             c_copy(i + 2).start()
 
-    t = lax.broadcasted_iota(jnp.int32, (QB, QB), 0)
-    s = lax.broadcasted_iota(jnp.int32, (QB, QB), 1)
+    hb = QB // 2
+    t = lax.broadcasted_iota(jnp.int32, (hb, hb), 1)
+    s = lax.broadcasted_iota(jnp.int32, (hb, hb), 0)
     tc = t // STRETCH
     sc = s // STRETCH
     masks[0] = jnp.where((tc == sc) & (s <= t), 1.0, 0.0).astype(F32)
-    for j in range(in_bits):
+    for j in range(in_bits - 1):
         hit = ((tc // 2**j) % 2 == 1) & (sc // 2**j == tc // 2**j - 1)
         masks[j + 1] = jnp.where(hit, 1.0, 0.0).astype(F32)
 
@@ -191,7 +187,7 @@
         level = []
         for b in range(n_b):
             at = pl.ds(b * QB, QB)
-            level.append(dot_tn(kv[0, at, cols], kv[1, at, cols]))
+            level.append(dot_tn(kv[1, at, cols], kv[0, at, cols]))
         base = 0
         while len(level) > 1:
             for b, state in enumerate(level):
@@ -257,32 +253,48 @@
             for h in range(heads):
                 cols = slice(h * HEAD_DIM, (h + 1) * HEAD_DIM)
                 qh = q[at, cols]
+                vh = kv[1, at, cols]
 
                 def weight(level):
-                    k = level * heads + h
-                    return lw_ref[at, k : k + 1]
-
-                scores = dot_nt(qh, kv[0, at, cols])
-                mix = weight(0) * masks[0]
-                for j in range(in_bits):
-                    mix = mix + weight(1 + j) * masks[1 + j]
-                left = [(scores * mix).astype(BF16)]
-                right = [kv[1, at, cols]]
-                qf = qh.astype(F32)
+                    return lw_ref[level, h : h + 1, at].astype(F32) * factors[level]
+
+                scores = dot_nt(kv[0, at, cols], qh)
+
+                def corner(lo):
+                    side = slice(lo, lo + hb)
+                    mix = weight(0)[:, side] * masks[0]
+                    for j in range(in_bits - 1):
+                        mix = mix + weight(1 + j)[:, side] * masks[1 + j]
+                    return (scores[side, side] * mix).astype(BF16)
+
+                upper = (scores[:hb, hb:] * weight(in_bits)[:, hb:]).astype(BF16)
+                probs = jnp.concatenate(
+                    [
+                        jnp.concatenate([corner(0), upper], 1),
+                        jnp.concatenate([jnp.zeros((hb, hb), BF16), corner(hb)], 1),
+                    ],
+                    0,
+                )
+                qt = qh.astype(F32).T
+                left = []
+                right = []
                 base = 0
                 for j in range(block_bits):
                     node = b // 2**j
                     bit = node % 2
-                    left.append((qf * (weight(n_in + j) * bit.astype(F32))).astype(BF16))
-                    right.append(local[base + node - bit, h])
+                    right.append((qt * (weight(n_in + j) * bit.astype(F32))).astype(BF16))
+                    left.append(local[base + node - bit, h])
                     base += n_b >> j
                 for j in range(seq_bits):
                     bit = (seq // 2**j) % 2
-                    left.append((qf * (weight(n_in + block_bits + j) * bit.astype(F32))).astype(BF16))
-                    right.append(rcv[j, h])
-                memory = dot(jnp.concatenate(left, 1), jnp.concatenate(right, 0))
-                mean = jnp.mean(memory * memory, axis=-1, keepdims=True)
-                att[at, cols] = (memory * lax.rsqrt(mean + 1e-06) * gate[at, cols]).astype(BF16)
+                    right.append((qt * (weight(n_in + block_bits + j) * bit.astype(F32))).astype(BF16))
+                    left.append(rcv[j, h])
+                memory = dot_tn(vh, probs) + dot(
+                    jnp.concatenate(left, 1), jnp.concatenate(right, 0)
+                )
+                mean = jnp.mean(memory * memory, axis=0, keepdims=True)
+                normed = (memory * lax.rsqrt(mean + 1e-06)).T
+                att[at, cols] = (normed * gate[at, cols]).astype(BF16)
 
         @pl.when(r > 0)
         def _():
@@ -353,20 +365,15 @@
     rows = rows_all // groups
     chips = groups // CORES
     spans = [STRETCH] + [STRETCH << j for j in range(levels - 1)]
-    factors = jnp.array([1.0 / 128.0 / math.sqrt(HEAD_DIM * span) for span in spans], F32)
-    level_weight = (level_codes.astype(F32) * factors[:, None, None]).reshape(
-        levels * heads, rows_all
-    ).T
-    scales = power_of_two(block_exponent + 16, 5) * jnp.float32(2.0 ** (-26))
-    scales = jnp.repeat(scales, BLOCK, axis=1)
+    factors = [1.0 / 128.0 / math.sqrt(HEAD_DIM * span) for span in spans]
     n_b = rows_all // QB
     vmem = pl.BlockSpec(memory_space=pltpu.VMEM)
     hbm = pl.BlockSpec(memory_space=pl.ANY)
     dma = pltpu.SemaphoreType.DMA
     return pl.pallas_call(
-        functools.partial(kernel, (groups, seq_bits, block_bits, in_bits)),
+        functools.partial(kernel, (groups, seq_bits, block_bits, in_bits, factors)),
         out_shape=jax.ShapeDtypeStruct((rows, depth), BF16),
-        in_specs=[hbm, hbm, hbm, vmem, vmem, vmem],
+        in_specs=[hbm, hbm, hbm, vmem, vmem, pl.BlockSpec(memory_space=pltpu.SMEM)],
         out_specs=vmem,
         scratch_shapes=[
             pltpu.VMEM((rows_all, depth), BF16),
@@ -383,7 +390,7 @@
             pltpu.VMEM((heads, HEAD_DIM, HEAD_DIM), F32),
             pltpu.VMEM((seq_bits, heads, HEAD_DIM, HEAD_DIM), BF16),
             pltpu.VMEM((seq_bits, heads, HEAD_DIM, HEAD_DIM), BF16),
-            pltpu.VMEM((1 + in_bits, QB, QB), F32),
+            pltpu.VMEM((in_bits, QB // 2, QB // 2), F32),
             pltpu.VMEM((rows, depth), F32),
             dma, dma((2,)), dma((2,)),
             dma((7 * chips - 6,)), dma((7 * chips - 6,)),
@@ -394,7 +401,7 @@
             collective_id=0, has_side_effects=True, vmem_limit_bytes=67043328
         ),
         name="layer",
-    )(tokens, w_proj, w_codes, gain.reshape(1, width), level_weight, scales)
+    )(tokens, w_proj, w_codes, gain.reshape(1, width), level_codes, block_exponent)
 
 
 def solution(mesh):

time: 84.3 us -> 76.6 us (0.909)
  Pallas kernels: 76.9 us -> 73.2 us
  local copies, waits for them, and re-layouts: 5.29 us -> 3.16 us
  other arithmetic: 1.78 us -> 0 us
    pallas_call x1, Pallas kernels: 76.9 us -> 73.2 us  [body(): pl.pallas_call(functools.partial(kernel, (groups, seq_bits, block_bits, i...]
    mul x2 -> x0, other arithmetic: 1.78 us -> none  [the longest x1 1.07 us: body(): level_codes.astype(F32) * factors[:, None, None]]
    reshape x2 -> x0, local copies, waits for them, and re-layouts: 1.44 us -> none  [body(): (level_codes.astype(F32) * factors[:, None, None]).reshape(levels * heads...]
    unnamed x3 -> x1, local copies, waits for them, and re-layouts: 3.85 us -> 3.16 us
where the time goes in v2:
time: 76.6 us; the launch traced here: 76.3 us
  Pallas kernels  73.2 us (96%)
  local copies, waits for them, and re-layouts  3.16 us (4%)
    pallas_call x1, Pallas kernels, body(): pl.pallas_call(functools.partial(kernel, (groups, seq_bits, block_bits, i...  73.2 us
    unnamed x1, local copies, waits for them, and re-layouts  3.16 us

profile of v2, /device:TPU:0, one launch (start us, length us, event | category | flops | bytes accessed | tf_op | source)
XLA Modules:
  0.0 76.3 jit_solution(5569335734308194167)
XLA Ops:
  0.0 73.2 %layer.1 = bf16[512,2048]{1,0:T(8,128)(2,1)} custom-call(bf16[2048,2048]{1,0:T(8,128)(2,1)} %tok_hbm.1, bf16[2048,4,512]{2,1,0:T(4,128)(2,1)} %w_hbm.1, s32[512,2048]{1,0:T(8,128)} %codes_hbm.1, f32[1,512]{1,0:T(1,128)} %bitcast.1, s32[9,4,2048]{2,1,0:T(4,128)} %lw_ref.1, s32[4,16]{1,0:T(4,128)} %scale_ref.1), custom_call_target="tpu_custom_call" | custom-call | tf_op jit(solution)/shard_map/layer/pallas_call | solution.py:373
  73.2 3.2 %copy.8 = bf16[512,2048]{1,0:T(8,128)(2,1)} copy(bf16[512,2048]{1,0:T(8,128)(2,1)} %layer.1) | data formatting | bytes 4194304

commit v3 on v2

--- a/solution.py
+++ b/solution.py
@@ -205,7 +205,6 @@
         )
 
     s_send(0).start()
-    relay(0)
 
     def exchange(j):
         s_send(j).wait_recv()
@@ -215,27 +214,35 @@
             snd[j + 1] = total.astype(BF16)
             s_send(j + 1).start()
 
+    in_loop = min(seq_bits - 1, n_t)
+
     @pl.loop(0, n_t)
     def _(i):
         at = pl.ds(pl.multiple_of(i * tb, tb), tb)
         q[at, :] = dot(tok[at, :], wj[0]).astype(BF16)
         g = dot(tok[at, :], wj[3])
         gate[at, :] = g / (1.0 + jnp.exp(-g)) * gain_ref[...]
-        for j in range(min(seq_bits, n_t)):
+        for j in range(in_loop):
             @pl.when(i == j)
             def _(j=j):
                 exchange(j)
-
-    for j in range(n_t, seq_bits):
+                if j == 0:
+                    relay(0)
+
+    if in_loop == 0:
+        relay(0)
+    relay(1)
+    for j in range(in_loop, seq_bits):
         exchange(j)
 
-    relay(1)
-
-    def a_send(r, target):
-        at = pl.ds(pl.multiple_of(target * rows, rows), rows)
+    n_parts = rows // QB
+
+    def a_send(r, target, part):
+        at = pl.ds(pl.multiple_of(target * rows + part * QB, QB), QB)
+        to = pl.ds(pl.multiple_of(part * QB, QB), QB)
         return pltpu.make_async_remote_copy(
-            src_ref=att.at[at], dst_ref=attr.at[mp],
-            send_sem=as_sem.at[r], recv_sem=ar_sem.at[r],
+            src_ref=att.at[at], dst_ref=attr.at[mp, to],
+            send_sem=as_sem.at[r * n_parts + part], recv_sem=ar_sem.at[r * n_parts + part],
             device_id=(seq, target), device_id_type=MESH,
         )
 
@@ -296,9 +303,9 @@
                 normed = (memory * lax.rsqrt(mean + 1e-06)).T
                 att[at, cols] = (normed * gate[at, cols]).astype(BF16)
 
-        @pl.when(r > 0)
-        def _():
-            a_send(r, owner).start()
+            @pl.when(r > 0)
+            def _():
+                a_send(r, owner, part).start()
 
     for ix in range(1, chips):
         for ch in range(2):
@@ -324,12 +331,14 @@
     for r in range(1, groups):
         ix, kc = r // CORES, r % CORES
         src = source(ix, kc)
-        at = pl.ds(pl.multiple_of(src * rows, rows), rows)
-        pltpu.make_async_remote_copy(
-            src_ref=att.at[own], dst_ref=attr.at[src],
-            send_sem=as_sem.at[r], recv_sem=ar_sem.at[r],
-            device_id=(seq, src), device_id_type=MESH,
-        ).wait_recv()
+        for part in range(n_parts):
+            to = pl.ds(part * QB, QB)
+            k = r * n_parts + part
+            pltpu.make_async_remote_copy(
+                src_ref=attr.at[src, to], dst_ref=attr.at[src, to],
+                send_sem=as_sem.at[k], recv_sem=ar_sem.at[k],
+                device_id=(seq, src), device_id_type=MESH,
+            ).wait_recv()
         if kc and ix:
             for ch in range(2):
                 cx_part(ix, ch, 1).wait_recv()
@@ -348,7 +357,8 @@
     for j in range(seq_bits):
         s_send(j).wait_send()
     for r in range(1, groups):
-        a_send(r, peer(r // CORES, r % CORES)).wait_send()
+        for part in range(n_parts):
+            a_send(r, peer(r // CORES, r % CORES), part).wait_send()
 
 
 def body(tokens, w_proj, gain, level_codes, w_codes, block_exponent):
@@ -394,7 +404,7 @@
             pltpu.VMEM((rows, depth), F32),
             dma, dma((2,)), dma((2,)),
             dma((7 * chips - 6,)), dma((7 * chips - 6,)),
-            dma((groups,)), dma((groups,)),
+            dma((groups * (rows // QB),)), dma((groups * (rows // QB),)),
             dma((seq_bits,)), dma((seq_bits,)),
         ],
         compiler_params=pltpu.CompilerParams(

time: 76.6 us -> 75.6 us (0.987)
  Pallas kernels: 73.2 us -> 72.2 us
    pallas_call x1, Pallas kernels: 73.2 us -> 72.2 us  [body(): pl.pallas_call(functools.partial(kernel, (groups, seq_bits, block_bits, i...]
where the time goes in v3:
time: 75.6 us; the launch traced here: 75.4 us
  Pallas kernels  72.2 us (96%)
  local copies, waits for them, and re-layouts  3.16 us (4%)
    pallas_call x1, Pallas kernels, body(): pl.pallas_call(functools.partial(kernel, (groups, seq_bits, block_bits, i...  72.2 us
    unnamed x1, local copies, waits for them, and re-layouts  3.16 us

profile of v3, /device:TPU:0, one launch (start us, length us, event | category | flops | bytes accessed | tf_op | source)
XLA Modules:
  0.0 75.4 jit_solution(8713726808036135486)
XLA Ops:
  0.0 72.2 %layer.1 = bf16[512,2048]{1,0:T(8,128)(2,1)} custom-call(bf16[2048,2048]{1,0:T(8,128)(2,1)} %tok_hbm.1, bf16[2048,4,512]{2,1,0:T(4,128)(2,1)} %w_hbm.1, s32[512,2048]{1,0:T(8,128)} %codes_hbm.1, f32[1,512]{1,0:T(1,128)} %bitcast.1, s32[9,4,2048]{2,1,0:T(4,128)} %lw_ref.1, s32[4,16]{1,0:T(4,128)} %scale_ref.1), custom_call_target="tpu_custom_call" | custom-call | tf_op jit(solution)/shard_map/layer/pallas_call | solution.py:383
  72.2 3.2 %copy.8 = bf16[512,2048]{1,0:T(8,128)(2,1)} copy(bf16[512,2048]{1,0:T(8,128)(2,1)} %layer.1) | data formatting | bytes 4194304
